TPU v7x, 32 devices: a whole 2x2x4 slice. The times are simulated.
32 devices in a mesh: group: 4 (over y, x), shard: 8 (over z, core).
Axes of the slice: x: 2, y: 2, z: 4, core: 2. Of those that a mesh axis runs over, the one named last changes fastest.
Arguments:
- queries: float32 [256, 768], P(('group', 'shard')), may hold values from -6 to 6
- codebook: float32 [96, 256, 8], replicated, may hold values from -0.21875 to 0.21875
- pq_codes: int32 [256, 96, 256], P(('group', 'shard')), may hold values from 0 to 255
- probes: int32 [256, 8], P('group'), may hold values from 0 to 63, all different within a row
- vectors: float32 [32768, 768], P(('group', 'shard')), may hold values from -0.21875 to 0.21875
- cand_owner: int32 [256, 16], P(('group', 'shard')), may hold values from 0 to 31, all different within a row; in each aligned block of 8 rows (0 to 7, 8 to 15, ...) at most 4 rows name the same one
- cand_row: int32 [256, 16], P(('group', 'shard')), may hold values from 0 to 1023
Outputs:
- pq_scores: float32 [256, 256, 64], P(('group', 'shard'))
- rerank_scores: float32 [256, 16], P(('group', 'shard'))
Inputs may be any that keep to these rules, and one draw needn't show every extreme that they name: The 8 probes of one query are distinct. `cand_owner`: the 16 owners of one query are distinct. Among the queries of one device no owner appears more than 4 times, and some owner appears exactly 4 times.
All inputs are finite; a program needn't handle non-finite values.
Results may differ from a plain program's by a relative error of at most 0.0029.
Values may be sent and summed in bfloat16 or wider, within the bound.
No kernel may reach another device: no remote copies, remote signals or barrier semaphores. Data moves between devices by JAX's collectives and lax.ppermute only.
A program may use at most 128 MiB of HBM per device.

v0:
```python
import jax
import jax.numpy as jnp
from jax import lax
from jax.sharding import PartitionSpec as P

M = 96
DS = 8
KS = 256


def build_tables(query_rows, codebook):
    number = query_rows.shape[0]
    pieces = query_rows.reshape(number, M, DS)
    tables = jnp.einsum("qmd,mkd->qmk", pieces, codebook, precision=lax.Precision.HIGHEST)
    return tables.reshape(number, M * KS).astype(jnp.bfloat16)


def score_lists(pq_codes, group_tables, probes, first_list):
    centres = jnp.arange(KS, dtype=jnp.int32)

    def one_list(inputs):
        list_codes, list_id = inputs
        onehot = (list_codes[:, None, :] == centres[None, :, None]).astype(jnp.bfloat16)
        onehot = onehot.reshape(M * KS, list_codes.shape[1])
        scores = lax.dot_general(
            onehot, group_tables, (((0,), (1,)), ((), ())), preferred_element_type=jnp.float32
        )
        probed = jnp.any(probes == list_id, axis=1)
        return jnp.where(probed[None, :], scores, 0.0)

    list_ids = first_list + jnp.arange(pq_codes.shape[0], dtype=jnp.int32)
    return lax.map(one_list, (pq_codes, list_ids))


def rerank(queries, vectors, cand_owner, cand_row):
    owners = lax.axis_size("group") * lax.axis_size("shard")
    pair_count = cand_owner.shape[0] * cand_owner.shape[1]
    capacity = max(2, pair_count // owners)
    owner_flat = cand_owner.reshape(pair_count)
    matches = (owner_flat[:, None] == jnp.arange(owners, dtype=jnp.int32)[None, :]).astype(
        jnp.int32
    )
    before = jnp.cumsum(matches, axis=0) - matches
    position = jnp.sum(before * matches, axis=1)
    target = owner_flat * capacity + position
    source = jnp.arange(pair_count, dtype=jnp.int32) // cand_owner.shape[1]
    send_rows = (
        jnp.zeros((owners * capacity, queries.shape[1]), jnp.float32)
        .at[target]
        .set(queries[source])
    )
    send_rows = send_rows.reshape(owners, capacity, queries.shape[1])
    send_ids = (
        jnp.full((owners * capacity,), -1.0, jnp.float32)
        .at[target]
        .set(cand_row.reshape(pair_count).astype(jnp.float32))
    )
    send_ids = send_ids.reshape(owners, capacity)
    rows_in = lax.all_to_all(send_rows, ("group", "shard"), split_axis=0, concat_axis=0, tiled=True)
    row_ids = lax.all_to_all(send_ids, ("group", "shard"), split_axis=0, concat_axis=0, tiled=True)
    filled = row_ids >= 0.0
    lookup = jnp.maximum(row_ids, 0.0).astype(jnp.int32)
    found = vectors[lookup]
    inner = jnp.einsum("snd,snd->sn", rows_in, found, precision=lax.Precision.HIGHEST)
    scored = jnp.where(filled, inner, 0.0)
    returned = lax.all_to_all(scored, ("group", "shard"), split_axis=0, concat_axis=0, tiled=True)
    result = returned.reshape(owners * capacity)[target]
    return result.reshape(cand_owner.shape)


def per_device(queries, codebook, pq_codes, probes, vectors, cand_owner, cand_row):
    first_list = lax.axis_index("shard") * pq_codes.shape[0]
    group_queries = lax.all_gather(queries, "shard", axis=0, tiled=True)
    group_tables = build_tables(group_queries, codebook)
    pq_scores = score_lists(pq_codes, group_tables, probes, first_list)
    rerank_scores = rerank(queries, vectors, cand_owner, cand_row)
    return (pq_scores, rerank_scores)


def solution(mesh):
    in_specs = (
        P(("group", "shard"), None),
        P(),
        P(("group", "shard"), None, None),
        P("group", None),
        P(("group", "shard"), None),
        P(("group", "shard"), None),
        P(("group", "shard"), None),
    )
    out_specs = (P(("group", "shard"), None, None), P(("group", "shard"), None))
    return jax.shard_map(
        per_device, mesh=mesh, in_specs=in_specs, out_specs=out_specs, check_vma=False
    )
```

profile of v0, /device:TPU:0, one launch (start us, length us, event | category | flops | bytes accessed | tf_op | source)
XLA Modules:
  0.0 161.3 jit_solution(348428554868212641)
XLA Ops:
  5.4 7.5 %all-to-all-start = ((f32[32,1,4]{2,1,0:T(1,128)}), f32[32,1,4]{2,1,0:T(1,128)}, u32[]{:S(2)}, u32[]{:S(2)}) async-start(f32[32,1,4]{2,1,0:T(1,128)} %bitcast.4), calls=%async_computation | async-start | bytes 32768 | tf_op jit(solution)/shard_map/all_to_all | solution.py:60
  12.8 15.7 %all_gather.3 = f32[64,768]{1,0:T(8,128)} all-gather(f32[8,768]{1,0:T(8,128)} %param.9), channel_id=1, replica_groups=mesh['group'=4,'shard'=8] {'shard'}, dimensions={0}, use_global_device_ids=true | all-gather | bytes 221184 | tf_op jit(solution)/shard_map/all_gather | solution.py:73
  29.7 7.5 %convert_bitcast_fusion = bf16[96,8,8,256]{3,2,1,0:T(8,128)(2,1)} fusion(f32[96,256,8]{1,2,0:T(8,128)} %param.10, f32[64,768]{0,1:T(8,128)S(1)} %copy.27), kind=kOutput, calls=%fused_computation.13 | convolution fusion | flops 152567808 | bytes 4128768 | tf_op jit(solution)/shard_map/qmd,mkd->qmk/dot_general | solution.py:14
  37.2 3.8 %copy.40 = bf16[96,8,8,256]{3,2,0,1:T(8,128)(2,1)} copy(bf16[96,8,8,256]{3,2,1,0:T(8,128)(2,1)} %convert_bitcast_fusion) | data formatting | bytes 6291456 | tf_op jit(solution)/shard_map/convert_element_type | solution.py:15
  44.8 5.4 %all-to-all-start.1 = ((f32[32,4,768]{2,1,0:T(4,128)}), f32[32,4,768]{2,1,0:T(4,128)S(1)}, u32[]{:S(2)}, u32[]{:S(2)}) async-start(f32[32,4,768]{2,1,0:T(4,128)} %reshape.135), calls=%async_computation.1 | async-start | bytes 786432 | tf_op jit(solution)/shard_map/all_to_all | solution.py:59
  50.3 84.8 %while.11 = (s32[]{:T(128)}, f32[8,256,64]{1,2,0:T(8,128)}, s32[8]{0:T(128)S(1)}, s32[64,8]{0,1:T(8,128)S(1)}, s32[8,96,256]{2,1,0:T(8,128)}, /*index=5*/bf16[64,24576]{1,0:T(8,128)(2,1)}, s32[]{:T(128)}) while((s32[]{:T(128)}, f32[8,256,64]{1,2,0:T(8,128)}, s32[8]{0:T(128)S(1)}, s32[64,8]{0,1:T(8,128)S(1)}, ...), condition=%wide.region_2.3_spmd.clone, body=%wide.region_0.2_spmd.clone.sunk | while | flops 811615168 | bytes 29067528 | solution.py:32
  51.5 4.3 %bitcast_compare_fusion.2 = pred[24576,256]{1,0:T(32,128)(4,1)S(1)} fusion(s32[24576]{0:T(1024)S(1)} %bitcast.56, s32[96,256]{1,0:T(8,128)S(1)} %dynamic-slice_bitcast_fusion.2), kind=kLoop, calls=%fused_computation.6.clone.1 | loop fusion | flops 6291456 | bytes 6488064 | tf_op jit(solution)/shard_map/while/body/eval_jaxpr/eq | solution.py:23
  57.0 3.9 %fusion.21 = f32[8,256,64]{1,2,0:T(8,128)} fusion(f32[8,256,64]{1,2,0:T(8,128)} %get-tuple-element.111, s32[]{:T(128)S(6)} %copy.46, pred[24576,256]{1,0:T(32,128)(4,1)S(1)} %bitcast_compare_fusion.2, bf16[64,24576]{1,0:T(8,128)(2,1)S(1)} %copy-done.1, pred[64]{0:T(512)(128)(4,1)S(1)} %compare_reduce_fusion.2), kind=kOutput, calls=%fused_computation.9.clone.1 | convolution fusion | flops 805322752 | bytes 9502788 | tf_op jit(solution)/shard_map/while/body/eval_jaxpr/dot_general | solution.py:25
  62.1 4.3 %bitcast_compare_fusion.2 = pred[24576,256]{1,0:T(32,128)(4,1)S(1)} fusion(s32[24576]{0:T(1024)S(1)} %bitcast.56, s32[96,256]{1,0:T(8,128)S(1)} %dynamic-slice_bitcast_fusion.2), kind=kLoop, calls=%fused_computation.6.clone.1 | loop fusion | flops 6291456 | bytes 6488064 | tf_op jit(solution)/shard_map/while/body/eval_jaxpr/eq | solution.py:23
  67.6 3.9 %fusion.21 = f32[8,256,64]{1,2,0:T(8,128)} fusion(f32[8,256,64]{1,2,0:T(8,128)} %get-tuple-element.111, s32[]{:T(128)S(6)} %copy.46, pred[24576,256]{1,0:T(32,128)(4,1)S(1)} %bitcast_compare_fusion.2, bf16[64,24576]{1,0:T(8,128)(2,1)S(1)} %copy-done.1, pred[64]{0:T(512)(128)(4,1)S(1)} %compare_reduce_fusion.2), kind=kOutput, calls=%fused_computation.9.clone.1 | convolution fusion | flops 805322752 | bytes 9502788 | tf_op jit(solution)/shard_map/while/body/eval_jaxpr/dot_general | solution.py:25
  72.7 4.3 %bitcast_compare_fusion.2 = pred[24576,256]{1,0:T(32,128)(4,1)S(1)} fusion(s32[24576]{0:T(1024)S(1)} %bitcast.56, s32[96,256]{1,0:T(8,128)S(1)} %dynamic-slice_bitcast_fusion.2), kind=kLoop, calls=%fused_computation.6.clone.1 | loop fusion | flops 6291456 | bytes 6488064 | tf_op jit(solution)/shard_map/while/body/eval_jaxpr/eq | solution.py:23
  78.2 3.9 %fusion.21 = f32[8,256,64]{1,2,0:T(8,128)} fusion(f32[8,256,64]{1,2,0:T(8,128)} %get-tuple-element.111, s32[]{:T(128)S(6)} %copy.46, pred[24576,256]{1,0:T(32,128)(4,1)S(1)} %bitcast_compare_fusion.2, bf16[64,24576]{1,0:T(8,128)(2,1)S(1)} %copy-done.1, pred[64]{0:T(512)(128)(4,1)S(1)} %compare_reduce_fusion.2), kind=kOutput, calls=%fused_computation.9.clone.1 | convolution fusion | flops 805322752 | bytes 9502788 | tf_op jit(solution)/shard_map/while/body/eval_jaxpr/dot_general | solution.py:25
  83.3 4.3 %bitcast_compare_fusion.2 = pred[24576,256]{1,0:T(32,128)(4,1)S(1)} fusion(s32[24576]{0:T(1024)S(1)} %bitcast.56, s32[96,256]{1,0:T(8,128)S(1)} %dynamic-slice_bitcast_fusion.2), kind=kLoop, calls=%fused_computation.6.clone.1 | loop fusion | flops 6291456 | bytes 6488064 | tf_op jit(solution)/shard_map/while/body/eval_jaxpr/eq | solution.py:23
  88.8 3.9 %fusion.21 = f32[8,256,64]{1,2,0:T(8,128)} fusion(f32[8,256,64]{1,2,0:T(8,128)} %get-tuple-element.111, s32[]{:T(128)S(6)} %copy.46, pred[24576,256]{1,0:T(32,128)(4,1)S(1)} %bitcast_compare_fusion.2, bf16[64,24576]{1,0:T(8,128)(2,1)S(1)} %copy-done.1, pred[64]{0:T(512)(128)(4,1)S(1)} %compare_reduce_fusion.2), kind=kOutput, calls=%fused_computation.9.clone.1 | convolution fusion | flops 805322752 | bytes 9502788 | tf_op jit(solution)/shard_map/while/body/eval_jaxpr/dot_general | solution.py:25
  93.8 4.3 %bitcast_compare_fusion.2 = pred[24576,256]{1,0:T(32,128)(4,1)S(1)} fusion(s32[24576]{0:T(1024)S(1)} %bitcast.56, s32[96,256]{1,0:T(8,128)S(1)} %dynamic-slice_bitcast_fusion.2), kind=kLoop, calls=%fused_computation.6.clone.1 | loop fusion | flops 6291456 | bytes 6488064 | tf_op jit(solution)/shard_map/while/body/eval_jaxpr/eq | solution.py:23
  99.4 3.9 %fusion.21 = f32[8,256,64]{1,2,0:T(8,128)} fusion(f32[8,256,64]{1,2,0:T(8,128)} %get-tuple-element.111, s32[]{:T(128)S(6)} %copy.46, pred[24576,256]{1,0:T(32,128)(4,1)S(1)} %bitcast_compare_fusion.2, bf16[64,24576]{1,0:T(8,128)(2,1)S(1)} %copy-done.1, pred[64]{0:T(512)(128)(4,1)S(1)} %compare_reduce_fusion.2), kind=kOutput, calls=%fused_computation.9.clone.1 | convolution fusion | flops 805322752 | bytes 9502788 | tf_op jit(solution)/shard_map/while/body/eval_jaxpr/dot_general | solution.py:25
  104.4 4.3 %bitcast_compare_fusion.2 = pred[24576,256]{1,0:T(32,128)(4,1)S(1)} fusion(s32[24576]{0:T(1024)S(1)} %bitcast.56, s32[96,256]{1,0:T(8,128)S(1)} %dynamic-slice_bitcast_fusion.2), kind=kLoop, calls=%fused_computation.6.clone.1 | loop fusion | flops 6291456 | bytes 6488064 | tf_op jit(solution)/shard_map/while/body/eval_jaxpr/eq | solution.py:23
  110.0 3.9 %fusion.21 = f32[8,256,64]{1,2,0:T(8,128)} fusion(f32[8,256,64]{1,2,0:T(8,128)} %get-tuple-element.111, s32[]{:T(128)S(6)} %copy.46, pred[24576,256]{1,0:T(32,128)(4,1)S(1)} %bitcast_compare_fusion.2, bf16[64,24576]{1,0:T(8,128)(2,1)S(1)} %copy-done.1, pred[64]{0:T(512)(128)(4,1)S(1)} %compare_reduce_fusion.2), kind=kOutput, calls=%fused_computation.9.clone.1 | convolution fusion | flops 805322752 | bytes 9502788 | tf_op jit(solution)/shard_map/while/body/eval_jaxpr/dot_general | solution.py:25
  115.0 4.3 %bitcast_compare_fusion.2 = pred[24576,256]{1,0:T(32,128)(4,1)S(1)} fusion(s32[24576]{0:T(1024)S(1)} %bitcast.56, s32[96,256]{1,0:T(8,128)S(1)} %dynamic-slice_bitcast_fusion.2), kind=kLoop, calls=%fused_computation.6.clone.1 | loop fusion | flops 6291456 | bytes 6488064 | tf_op jit(solution)/shard_map/while/body/eval_jaxpr/eq | solution.py:23
  120.6 3.9 %fusion.21 = f32[8,256,64]{1,2,0:T(8,128)} fusion(f32[8,256,64]{1,2,0:T(8,128)} %get-tuple-element.111, s32[]{:T(128)S(6)} %copy.46, pred[24576,256]{1,0:T(32,128)(4,1)S(1)} %bitcast_compare_fusion.2, bf16[64,24576]{1,0:T(8,128)(2,1)S(1)} %copy-done.1, pred[64]{0:T(512)(128)(4,1)S(1)} %compare_reduce_fusion.2), kind=kOutput, calls=%fused_computation.9.clone.1 | convolution fusion | flops 805322752 | bytes 9502788 | tf_op jit(solution)/shard_map/while/body/eval_jaxpr/dot_general | solution.py:25
  125.6 4.3 %bitcast_compare_fusion.2 = pred[24576,256]{1,0:T(32,128)(4,1)S(1)} fusion(s32[24576]{0:T(1024)S(1)} %bitcast.56, s32[96,256]{1,0:T(8,128)S(1)} %dynamic-slice_bitcast_fusion.2), kind=kLoop, calls=%fused_computation.6.clone.1 | loop fusion | flops 6291456 | bytes 6488064 | tf_op jit(solution)/shard_map/while/body/eval_jaxpr/eq | solution.py:23
  131.2 3.9 %fusion.21 = f32[8,256,64]{1,2,0:T(8,128)} fusion(f32[8,256,64]{1,2,0:T(8,128)} %get-tuple-element.111, s32[]{:T(128)S(6)} %copy.46, pred[24576,256]{1,0:T(32,128)(4,1)S(1)} %bitcast_compare_fusion.2, bf16[64,24576]{1,0:T(8,128)(2,1)S(1)} %copy-done.1, pred[64]{0:T(512)(128)(4,1)S(1)} %compare_reduce_fusion.2), kind=kOutput, calls=%fused_computation.9.clone.1 | convolution fusion | flops 805322752 | bytes 9502788 | tf_op jit(solution)/shard_map/while/body/eval_jaxpr/dot_general | solution.py:25
  145.1 5.8 %all-to-all-start.2 = ((f32[32,1,4]{2,1,0:T(1,128)}), f32[32,1,4]{2,1,0:T(1,128)S(1)}, u32[]{:S(2)}, u32[]{:S(2)}) async-start(f32[32,1,4]{2,1,0:T(1,128)} %copy.33), calls=%async_computation.2 | async-start | bytes 32768 | tf_op jit(solution)/shard_map/all_to_all | solution.py:66
  151.6 6.5 %all-to-all-done.2 = f32[32,1,4]{2,1,0:T(1,128)S(1)} async-done(((f32[32,1,4]{2,1,0:T(1,128)}), f32[32,1,4]{2,1,0:T(1,128)S(1)}, u32[]{:S(2)}, u32[]{:S(2)}) %all-to-all-start.2) | async-done | bytes 544 | tf_op jit(solution)/shard_map/all_to_all | solution.py:66
  (101 shorter events, 42.7 us)
Async XLA Ops:
  0.6 138.5 %copy-start = (f32[1024,768]{1,0:T(8,128)S(1)}, f32[1024,768]{1,0:T(8,128)}, u32[]{:S(2)}) copy-start(f32[1024,768]{1,0:T(8,128)} %param.13) | copy-start | bytes 9437188
  3.7 41.2 %copy-start.4 = (s32[128]{0:T(128)}, s32[128]{0:T(128)S(1)}, u32[]{:S(2)}) copy-start(s32[128]{0:T(128)S(1)} %fusion.10) | copy-start | bytes 1540
  5.4 39.5 %all-to-all-start = ((f32[32,1,4]{2,1,0:T(1,128)}), f32[32,1,4]{2,1,0:T(1,128)}, u32[]{:S(2)}, u32[]{:S(2)}) async-start(f32[32,1,4]{2,1,0:T(1,128)} %bitcast.4), calls=%async_computation | async-start | bytes 32768 | tf_op jit(solution)/shard_map/all_to_all | solution.py:60
  29.7 20.6 %copy-start.2 = (s32[64,8]{0,1:T(8,128)S(1)}, s32[64,8]{0,1:T(8,128)}, u32[]{:S(2)}) copy-start(s32[64,8]{0,1:T(8,128)} %param.12) | copy-start | bytes 6148
  44.8 97.7 %all-to-all-start.1 = ((f32[32,4,768]{2,1,0:T(4,128)}), f32[32,4,768]{2,1,0:T(4,128)S(1)}, u32[]{:S(2)}, u32[]{:S(2)}) async-start(f32[32,4,768]{2,1,0:T(4,128)} %reshape.135), calls=%async_computation.1 | async-start | bytes 786432 | tf_op jit(solution)/shard_map/all_to_all | solution.py:59
  50.3 6.7 %copy-start.1 = (bf16[64,24576]{1,0:T(8,128)(2,1)S(1)}, bf16[64,24576]{1,0:T(8,128)(2,1)}, u32[]{:S(2)}) copy-start(bf16[64,24576]{1,0:T(8,128)(2,1)} %get-tuple-element.122) | copy-start | bytes 9437188 | tf_op jit(solution)/shard_map/while
  60.9 6.7 %copy-start.1 = (bf16[64,24576]{1,0:T(8,128)(2,1)S(1)}, bf16[64,24576]{1,0:T(8,128)(2,1)}, u32[]{:S(2)}) copy-start(bf16[64,24576]{1,0:T(8,128)(2,1)} %get-tuple-element.122) | copy-start | bytes 9437188 | tf_op jit(solution)/shard_map/while
  71.5 6.7 %copy-start.1 = (bf16[64,24576]{1,0:T(8,128)(2,1)S(1)}, bf16[64,24576]{1,0:T(8,128)(2,1)}, u32[]{:S(2)}) copy-start(bf16[64,24576]{1,0:T(8,128)(2,1)} %get-tuple-element.122) | copy-start | bytes 9437188 | tf_op jit(solution)/shard_map/while
  82.1 6.7 %copy-start.1 = (bf16[64,24576]{1,0:T(8,128)(2,1)S(1)}, bf16[64,24576]{1,0:T(8,128)(2,1)}, u32[]{:S(2)}) copy-start(bf16[64,24576]{1,0:T(8,128)(2,1)} %get-tuple-element.122) | copy-start | bytes 9437188 | tf_op jit(solution)/shard_map/while
  92.7 6.7 %copy-start.1 = (bf16[64,24576]{1,0:T(8,128)(2,1)S(1)}, bf16[64,24576]{1,0:T(8,128)(2,1)}, u32[]{:S(2)}) copy-start(bf16[64,24576]{1,0:T(8,128)(2,1)} %get-tuple-element.122) | copy-start | bytes 9437188 | tf_op jit(solution)/shard_map/while
  103.3 6.7 %copy-start.1 = (bf16[64,24576]{1,0:T(8,128)(2,1)S(1)}, bf16[64,24576]{1,0:T(8,128)(2,1)}, u32[]{:S(2)}) copy-start(bf16[64,24576]{1,0:T(8,128)(2,1)} %get-tuple-element.122) | copy-start | bytes 9437188 | tf_op jit(solution)/shard_map/while
  113.9 6.7 %copy-start.1 = (bf16[64,24576]{1,0:T(8,128)(2,1)S(1)}, bf16[64,24576]{1,0:T(8,128)(2,1)}, u32[]{:S(2)}) copy-start(bf16[64,24576]{1,0:T(8,128)(2,1)} %get-tuple-element.122) | copy-start | bytes 9437188 | tf_op jit(solution)/shard_map/while
  124.5 6.7 %copy-start.1 = (bf16[64,24576]{1,0:T(8,128)(2,1)S(1)}, bf16[64,24576]{1,0:T(8,128)(2,1)}, u32[]{:S(2)}) copy-start(bf16[64,24576]{1,0:T(8,128)(2,1)} %get-tuple-element.122) | copy-start | bytes 9437188 | tf_op jit(solution)/shard_map/while
  135.9 0.6 copy-start.3
  145.1 13.0 %all-to-all-start.2 = ((f32[32,1,4]{2,1,0:T(1,128)}), f32[32,1,4]{2,1,0:T(1,128)S(1)}, u32[]{:S(2)}, u32[]{:S(2)}) async-start(f32[32,1,4]{2,1,0:T(1,128)} %copy.33), calls=%async_computation.2 | async-start | bytes 32768 | tf_op jit(solution)/shard_map/all_to_all | solution.py:66
where the time goes:
time: 162 us; the launch traced here: 161 us
  other arithmetic  45.8 us (28%)
  matrix products  38.9 us (24%)
  local copies, waits for them, and re-layouts  34.8 us (21%)
  starting transfers between devices  18.7 us (12%)
  blocking collectives  15.7 us (10%)
  waiting for transfers between devices  6.5 us (4%)
    eq x8, other arithmetic, one_list(): list_codes[:, None, :] == centres[None, :, None]  34.1 us
    dot_general x8, matrix products, one_list(): lax.dot_general(onehot, group_tables, (((0,), (1,)), ((), ())), preferred...  31.3 us
    all_gather x1, blocking collectives, per_device(): group_queries = lax.all_gather(queries, 'shard', axis=0, tiled=True)  15.7 us
    eq x8, local copies, waits for them, and re-layouts, one_list(): list_codes[:, None, :] == centres[None, :, None]  8.45 us
    dot_general x1, matrix products, build_tables(): jnp.einsum('qmd,mkd->qmk', pieces, codebook, precision=lax.Precision.HIGH...  7.55 us
    all_to_all x1, starting transfers between devices, rerank(): lax.all_to_all(send_ids, ('group', 'shard'), split_axis=0, concat_axis=0,...  7.45 us
    all_to_all x1, waiting for transfers between devices, rerank(): lax.all_to_all(scored, ('group', 'shard'), split_axis=0, concat_axis=0, t...  6.49 us
    all_to_all x1, starting transfers between devices, rerank(): lax.all_to_all(scored, ('group', 'shard'), split_axis=0, concat_axis=0, t...  5.83 us
  transfers between devices with their start and end apart: 3, of which 1 were waited for; matrix products, arithmetic and copies ran while one was open for 67% of the time, Pallas kernels for 0%

commit v1 on v0

--- a/solution.py
+++ b/solution.py
@@ -70,7 +70,14 @@
 
 def per_device(queries, codebook, pq_codes, probes, vectors, cand_owner, cand_row):
     first_list = lax.axis_index("shard") * pq_codes.shape[0]
-    group_queries = lax.all_gather(queries, "shard", axis=0, tiled=True)
+    ring = [queries]
+    for hop in range(7):
+        ring.append(lax.ppermute(ring[-1], "shard", [(dev, (dev + 1) % 8) for dev in range(8)]))
+    group_queries = jnp.roll(
+        jnp.concatenate(ring[::-1], axis=0),
+        (lax.axis_index("shard") + 1) * ring[0].shape[0],
+        axis=0,
+    )
     group_tables = build_tables(group_queries, codebook)
     pq_scores = score_lists(pq_codes, group_tables, probes, first_list)
     rerank_scores = rerank(queries, vectors, cand_owner, cand_row)

time: 162 us -> 172 us (1.062)
  waiting for transfers between devices: 6.5 us -> 22.7 us
  blocking collectives: 15.7 us -> 0 us
  local copies, waits for them, and re-layouts: 34.8 us -> 43.5 us
    ppermute x0 -> x7, waiting for transfers between devices: none -> 22.7 us  [per_device(): lax.ppermute(ring[-1], 'shard', [(dev, (dev + 1) % 8) for dev in range(8)])]
    all_gather x1 -> x0, blocking collectives: 15.7 us -> none  [per_device(): group_queries = lax.all_gather(queries, 'shard', axis=0, tiled=True)]
    unnamed x8 -> x33, local copies, waits for them, and re-layouts: 0.61 us -> 11.1 us
    all_to_all x1, waiting for transfers between devices: 6.49 us -> 0.01 us  [rerank(): lax.all_to_all(scored, ('group', 'shard'), split_axis=0, concat_axis=0, t...]
    dynamic_slice x0 -> x2, local copies, waits for them, and re-layouts: none -> 2.55 us  [per_device(): jnp.roll(jnp.concatenate(ring[::-1], axis=0), (lax.axis_index('shard') +...]
    convert_element_type x1, local copies, waits for them, and re-layouts: 3.76 us -> 1.85 us  [build_tables(): return tables.reshape(number, M * KS).astype(jnp.bfloat16)]
    reduce_or x8, other arithmetic: 5.23 us -> 6.95 us  [one_list(): probed = jnp.any(probes == list_id, axis=1)]
  transfers between devices with their start and end apart: 3 -> 10, of which waited for: 1 -> 5; matrix products, arithmetic and copies ran while one was open for 67% -> 71% of each run, Pallas kernels for 0% -> 0%
where the time goes in v1:
time: 172 us; the launch traced here: 171 us
  other arithmetic  46.4 us (27%)
  local copies, waits for them, and re-layouts  43.5 us (25%)
  matrix products  37.7 us (22%)
  waiting for transfers between devices  22.7 us (13%)
  starting transfers between devices  19.3 us (11%)
    eq x8, other arithmetic, one_list(): list_codes[:, None, :] == centres[None, :, None]  34.6 us
    dot_general x8, matrix products, one_list(): lax.dot_general(onehot, group_tables, (((0,), (1,)), ((), ())), preferred...  31.3 us
    ppermute x7, waiting for transfers between devices, per_device(): lax.ppermute(ring[-1], 'shard', [(dev, (dev + 1) % 8) for dev in range(8)])  22.7 us
    unnamed x33, local copies, waits for them, and re-layouts  11.1 us
    eq x8, local copies, waits for them, and re-layouts, one_list(): list_codes[:, None, :] == centres[None, :, None]  7.22 us
    reduce_or x8, other arithmetic, one_list(): probed = jnp.any(probes == list_id, axis=1)  6.95 us
    dot_general x1, matrix products, build_tables(): jnp.einsum('qmd,mkd->qmk', pieces, codebook, precision=lax.Precision.HIGH...  6.36 us
    all_to_all x1, starting transfers between devices, rerank(): lax.all_to_all(send_ids, ('group', 'shard'), split_axis=0, concat_axis=0,...  6.27 us
  transfers between devices with their start and end apart: 10, of which 5 were waited for; matrix products, arithmetic and copies ran while one was open for 71% of the time, Pallas kernels for 0%

profile of v1, /device:TPU:0, one launch (start us, length us, event | category | flops | bytes accessed | tf_op | source)
XLA Modules:
  0.0 170.6 jit_solution(16261544470545428488)
XLA Ops:
  9.4 6.3 %all-to-all-start = ((f32[32,1,4]{2,1,0:T(1,128)}), f32[32,1,4]{2,1,0:T(1,128)S(1)}, u32[]{:S(2)}, u32[]{:S(2)}) async-start(f32[32,1,4]{2,1,0:T(1,128)} %bitcast.4), calls=%async_computation | async-start | bytes 32768 | tf_op jit(solution)/shard_map/all_to_all | solution.py:60
  16.0 4.8 %collective-permute-done.2 = f32[8,768]{1,0:T(8,128)S(1)} collective-permute-done((f32[8,768]{1,0:T(8,128)S(1)}, f32[8,768]{1,0:T(8,128)S(1)}, u32[]{:S(2)}, u32[]{:S(2)}) %collective-permute-start.2) | collective-permute-done | bytes 24608 | tf_op jit(solution)/shard_map/ppermute | solution.py:75
  20.9 5.0 %collective-permute-done.3 = f32[8,768]{1,0:T(8,128)S(1)} collective-permute-done((f32[8,768]{1,0:T(8,128)S(1)}, f32[8,768]{1,0:T(8,128)S(1)}, u32[]{:S(2)}, u32[]{:S(2)}) %collective-permute-start.3) | collective-permute-done | bytes 24608 | tf_op jit(solution)/shard_map/ppermute | solution.py:75
  26.6 4.4 %collective-permute-done.4 = f32[8,768]{1,0:T(8,128)S(1)} collective-permute-done((f32[8,768]{1,0:T(8,128)S(1)}, f32[8,768]{1,0:T(8,128)S(1)}, u32[]{:S(2)}, u32[]{:S(2)}) %collective-permute-start.4) | collective-permute-done | bytes 24608 | tf_op jit(solution)/shard_map/ppermute | solution.py:75
  31.2 4.9 %collective-permute-done.5 = f32[8,768]{1,0:T(8,128)} collective-permute-done((f32[8,768]{1,0:T(8,128)S(1)}, f32[8,768]{1,0:T(8,128)}, u32[]{:S(2)}, u32[]{:S(2)}) %collective-permute-start.5) | collective-permute-done | bytes 24608 | tf_op jit(solution)/shard_map/ppermute | solution.py:75
  40.4 6.1 %all-to-all-start.1 = ((f32[32,4,768]{2,1,0:T(4,128)}), f32[32,4,768]{2,1,0:T(4,128)S(1)}, u32[]{:S(2)}, u32[]{:S(2)}) async-start(f32[32,4,768]{2,1,0:T(4,128)} %reshape.135), calls=%async_computation.1 | async-start | bytes 786432 | tf_op jit(solution)/shard_map/all_to_all | solution.py:59
  64.4 6.4 %convert_bitcast_fusion = bf16[96,8,8,256]{3,2,1,0:T(8,128)(2,1)S(1)} fusion(f32[96,256,8]{1,2,0:T(8,128)} %param.10, f32[64,768]{0,1:T(8,128)} %copy.27), kind=kOutput, calls=%fused_computation.13 | convolution fusion | flops 152567808 | bytes 4128768 | tf_op jit(solution)/shard_map/qmd,mkd->qmk/dot_general | solution.py:14
  75.9 6.0 %all-to-all-start.2 = ((f32[32,1,4]{2,1,0:T(1,128)}), f32[32,1,4]{2,1,0:T(1,128)S(1)}, u32[]{:S(2)}, u32[]{:S(2)}) async-start(f32[32,1,4]{2,1,0:T(1,128)} %copy.33), calls=%async_computation.2 | async-start | bytes 32768 | tf_op jit(solution)/shard_map/all_to_all | solution.py:66
  81.9 85.5 %while.11 = (s32[]{:T(128)}, f32[8,256,64]{1,2,0:T(8,128)}, s32[8]{0:T(128)S(1)}, s32[64,8]{0,1:T(8,128)S(1)}, s32[8,96,256]{2,1,0:T(8,128)}, /*index=5*/bf16[64,24576]{1,0:T(8,128)(2,1)}, s32[]{:T(128)}) while((s32[]{:T(128)}, f32[8,256,64]{1,2,0:T(8,128)}, s32[8]{0:T(128)S(1)}, s32[64,8]{0,1:T(8,128)S(1)}, ...), condition=%wide.region_2.3_spmd.clone, body=%wide.region_0.2_spmd.clone.sunk | while | flops 811615168 | bytes 29068028 | solution.py:32
  84.4 4.3 %bitcast_compare_fusion.2 = pred[24576,256]{1,0:T(32,128)(4,1)S(1)} fusion(s32[24576]{0:T(1024)S(1)} %bitcast.56, s32[96,256]{1,0:T(8,128)S(1)} %dynamic-slice_bitcast_fusion.2), kind=kLoop, calls=%fused_computation.6.clone.1 | loop fusion | flops 6291456 | bytes 6488064 | tf_op jit(solution)/shard_map/while/body/eval_jaxpr/eq | solution.py:23
  88.7 3.9 %fusion.21 = f32[8,256,64]{1,2,0:T(8,128)} fusion(f32[8,256,64]{1,2,0:T(8,128)} %get-tuple-element.113, s32[]{:T(128)} %get-tuple-element.112, pred[24576,256]{1,0:T(32,128)(4,1)S(1)} %bitcast_compare_fusion.2, bf16[64,24576]{1,0:T(8,128)(2,1)S(1)} %copy-done.1, pred[64]{0:T(512)(128)(4,1)S(1)} %compare_reduce_fusion.2), kind=kOutput, calls=%fused_computation.9.clone.1 | convolution fusion | flops 805322752 | bytes 9503296 | tf_op jit(solution)/shard_map/while/body/eval_jaxpr/dot_general | solution.py:25
  95.0 4.3 %bitcast_compare_fusion.2 = pred[24576,256]{1,0:T(32,128)(4,1)S(1)} fusion(s32[24576]{0:T(1024)S(1)} %bitcast.56, s32[96,256]{1,0:T(8,128)S(1)} %dynamic-slice_bitcast_fusion.2), kind=kLoop, calls=%fused_computation.6.clone.1 | loop fusion | flops 6291456 | bytes 6488064 | tf_op jit(solution)/shard_map/while/body/eval_jaxpr/eq | solution.py:23
  99.4 3.9 %fusion.21 = f32[8,256,64]{1,2,0:T(8,128)} fusion(f32[8,256,64]{1,2,0:T(8,128)} %get-tuple-element.113, s32[]{:T(128)} %get-tuple-element.112, pred[24576,256]{1,0:T(32,128)(4,1)S(1)} %bitcast_compare_fusion.2, bf16[64,24576]{1,0:T(8,128)(2,1)S(1)} %copy-done.1, pred[64]{0:T(512)(128)(4,1)S(1)} %compare_reduce_fusion.2), kind=kOutput, calls=%fused_computation.9.clone.1 | convolution fusion | flops 805322752 | bytes 9503296 | tf_op jit(solution)/shard_map/while/body/eval_jaxpr/dot_general | solution.py:25
  105.7 4.3 %bitcast_compare_fusion.2 = pred[24576,256]{1,0:T(32,128)(4,1)S(1)} fusion(s32[24576]{0:T(1024)S(1)} %bitcast.56, s32[96,256]{1,0:T(8,128)S(1)} %dynamic-slice_bitcast_fusion.2), kind=kLoop, calls=%fused_computation.6.clone.1 | loop fusion | flops 6291456 | bytes 6488064 | tf_op jit(solution)/shard_map/while/body/eval_jaxpr/eq | solution.py:23
  110.1 3.9 %fusion.21 = f32[8,256,64]{1,2,0:T(8,128)} fusion(f32[8,256,64]{1,2,0:T(8,128)} %get-tuple-element.113, s32[]{:T(128)} %get-tuple-element.112, pred[24576,256]{1,0:T(32,128)(4,1)S(1)} %bitcast_compare_fusion.2, bf16[64,24576]{1,0:T(8,128)(2,1)S(1)} %copy-done.1, pred[64]{0:T(512)(128)(4,1)S(1)} %compare_reduce_fusion.2), kind=kOutput, calls=%fused_computation.9.clone.1 | convolution fusion | flops 805322752 | bytes 9503296 | tf_op jit(solution)/shard_map/while/body/eval_jaxpr/dot_general | solution.py:25
  116.4 4.3 %bitcast_compare_fusion.2 = pred[24576,256]{1,0:T(32,128)(4,1)S(1)} fusion(s32[24576]{0:T(1024)S(1)} %bitcast.56, s32[96,256]{1,0:T(8,128)S(1)} %dynamic-slice_bitcast_fusion.2), kind=kLoop, calls=%fused_computation.6.clone.1 | loop fusion | flops 6291456 | bytes 6488064 | tf_op jit(solution)/shard_map/while/body/eval_jaxpr/eq | solution.py:23
  120.7 3.9 %fusion.21 = f32[8,256,64]{1,2,0:T(8,128)} fusion(f32[8,256,64]{1,2,0:T(8,128)} %get-tuple-element.113, s32[]{:T(128)} %get-tuple-element.112, pred[24576,256]{1,0:T(32,128)(4,1)S(1)} %bitcast_compare_fusion.2, bf16[64,24576]{1,0:T(8,128)(2,1)S(1)} %copy-done.1, pred[64]{0:T(512)(128)(4,1)S(1)} %compare_reduce_fusion.2), kind=kOutput, calls=%fused_computation.9.clone.1 | convolution fusion | flops 805322752 | bytes 9503296 | tf_op jit(solution)/shard_map/while/body/eval_jaxpr/dot_general | solution.py:25
  127.1 4.3 %bitcast_compare_fusion.2 = pred[24576,256]{1,0:T(32,128)(4,1)S(1)} fusion(s32[24576]{0:T(1024)S(1)} %bitcast.56, s32[96,256]{1,0:T(8,128)S(1)} %dynamic-slice_bitcast_fusion.2), kind=kLoop, calls=%fused_computation.6.clone.1 | loop fusion | flops 6291456 | bytes 6488064 | tf_op jit(solution)/shard_map/while/body/eval_jaxpr/eq | solution.py:23
  131.4 3.9 %fusion.21 = f32[8,256,64]{1,2,0:T(8,128)} fusion(f32[8,256,64]{1,2,0:T(8,128)} %get-tuple-element.113, s32[]{:T(128)} %get-tuple-element.112, pred[24576,256]{1,0:T(32,128)(4,1)S(1)} %bitcast_compare_fusion.2, bf16[64,24576]{1,0:T(8,128)(2,1)S(1)} %copy-done.1, pred[64]{0:T(512)(128)(4,1)S(1)} %compare_reduce_fusion.2), kind=kOutput, calls=%fused_computation.9.clone.1 | convolution fusion | flops 805322752 | bytes 9503296 | tf_op jit(solution)/shard_map/while/body/eval_jaxpr/dot_general | solution.py:25
  137.8 4.3 %bitcast_compare_fusion.2 = pred[24576,256]{1,0:T(32,128)(4,1)S(1)} fusion(s32[24576]{0:T(1024)S(1)} %bitcast.56, s32[96,256]{1,0:T(8,128)S(1)} %dynamic-slice_bitcast_fusion.2), kind=kLoop, calls=%fused_computation.6.clone.1 | loop fusion | flops 6291456 | bytes 6488064 | tf_op jit(solution)/shard_map/while/body/eval_jaxpr/eq | solution.py:23
  148.5 4.3 %bitcast_compare_fusion.2 = pred[24576,256]{1,0:T(32,128)(4,1)S(1)} fusion(s32[24576]{0:T(1024)S(1)} %bitcast.56, s32[96,256]{1,0:T(8,128)S(1)} %dynamic-slice_bitcast_fusion.2), kind=kLoop, calls=%fused_computation.6.clone.1 | loop fusion | flops 6291456 | bytes 6488064 | tf_op jit(solution)/shard_map/while/body/eval_jaxpr/eq | solution.py:23
  152.8 3.9 %fusion.21 = f32[8,256,64]{1,2,0:T(8,128)} fusion(f32[8,256,64]{1,2,0:T(8,128)} %get-tuple-element.113, s32[]{:T(128)} %get-tuple-element.112, pred[24576,256]{1,0:T(32,128)(4,1)S(1)} %bitcast_compare_fusion.2, bf16[64,24576]{1,0:T(8,128)(2,1)S(1)} %copy-done.1, pred[64]{0:T(512)(128)(4,1)S(1)} %compare_reduce_fusion.2), kind=kOutput, calls=%fused_computation.9.clone.1 | convolution fusion | flops 805322752 | bytes 9503296 | tf_op jit(solution)/shard_map/while/body/eval_jaxpr/dot_general | solution.py:25
  159.1 4.3 %bitcast_compare_fusion.2 = pred[24576,256]{1,0:T(32,128)(4,1)S(1)} fusion(s32[24576]{0:T(1024)S(1)} %bitcast.56, s32[96,256]{1,0:T(8,128)S(1)} %dynamic-slice_bitcast_fusion.2), kind=kLoop, calls=%fused_computation.6.clone.1 | loop fusion | flops 6291456 | bytes 6488064 | tf_op jit(solution)/shard_map/while/body/eval_jaxpr/eq | solution.py:23
  163.5 3.9 %fusion.21 = f32[8,256,64]{1,2,0:T(8,128)} fusion(f32[8,256,64]{1,2,0:T(8,128)} %get-tuple-element.113, s32[]{:T(128)} %get-tuple-element.112, pred[24576,256]{1,0:T(32,128)(4,1)S(1)} %bitcast_compare_fusion.2, bf16[64,24576]{1,0:T(8,128)(2,1)S(1)} %copy-done.1, pred[64]{0:T(512)(128)(4,1)S(1)} %compare_reduce_fusion.2), kind=kOutput, calls=%fused_computation.9.clone.1 | convolution fusion | flops 805322752 | bytes 9503296 | tf_op jit(solution)/shard_map/while/body/eval_jaxpr/dot_general | solution.py:25
  (140 shorter events, 63.6 us)
Async XLA Ops:
  0.6 45.9 %copy-start = (f32[1024,768]{1,0:T(8,128)S(1)}, f32[1024,768]{1,0:T(8,128)}, u32[]{:S(2)}) copy-start(f32[1024,768]{1,0:T(8,128)} %param.13) | copy-start | bytes 9437188
  0.6 6.3 %collective-permute-start = (f32[8,768]{1,0:T(8,128)}, f32[8,768]{1,0:T(8,128)S(1)}, u32[]{:S(2)}, u32[]{:S(2)}) collective-permute-start(f32[8,768]{1,0:T(8,128)} %param.9), channel_id=1, source_target_pairs={{0,1},{1,2},{2,3},{3,4},{4,5},{5,6},{6,7},{7,0},{8,9},{9,10},{10,1... | collective-permute-start | bytes 73736 | tf_op jit(solution)/shard_map/ppermute | solution.py:75
  6.9 29.2 %copy-start.3 = (f32[8,768]{1,0:T(8,128)}, f32[8,768]{1,0:T(8,128)S(1)}, u32[]{:S(2)}) copy-start(f32[8,768]{1,0:T(8,128)S(1)} %collective-permute-done) | copy-start | bytes 73732
  6.9 8.8 %collective-permute-start.1 = (f32[8,768]{1,0:T(8,128)S(1)}, f32[8,768]{1,0:T(8,128)S(1)}, u32[]{:S(2)}, u32[]{:S(2)}) collective-permute-start(f32[8,768]{1,0:T(8,128)S(1)} %collective-permute-done), channel_id=1, source_target_pairs={{0,1},{1,2},{2,3},{3,4},{4,5},{5,6},{6,7},{7,0},{8,9},{9,10},{10,1... | collective-permute-start | bytes 73736 | tf_op jit(solution)/shard_map/ppermute | solution.py:75
  7.0 24.0 %copy-start.8 = (s32[128]{0:T(128)}, s32[128]{0:T(128)S(1)}, u32[]{:S(2)}) copy-start(s32[128]{0:T(128)S(1)} %fusion.10) | copy-start | bytes 1540
  9.4 17.1 %all-to-all-start = ((f32[32,1,4]{2,1,0:T(1,128)}), f32[32,1,4]{2,1,0:T(1,128)S(1)}, u32[]{:S(2)}, u32[]{:S(2)}) async-start(f32[32,1,4]{2,1,0:T(1,128)} %bitcast.4), calls=%async_computation | async-start | bytes 32768 | tf_op jit(solution)/shard_map/all_to_all | solution.py:60
  15.7 20.4 %copy-start.4 = (f32[8,768]{1,0:T(8,128)}, f32[8,768]{1,0:T(8,128)S(1)}, u32[]{:S(2)}) copy-start(f32[8,768]{1,0:T(8,128)S(1)} %collective-permute-done.1) | copy-start | bytes 73732
  15.7 5.1 %collective-permute-start.2 = (f32[8,768]{1,0:T(8,128)S(1)}, f32[8,768]{1,0:T(8,128)S(1)}, u32[]{:S(2)}, u32[]{:S(2)}) collective-permute-start(f32[8,768]{1,0:T(8,128)S(1)} %collective-permute-done.1), channel_id=1, source_target_pairs={{0,1},{1,2},{2,3},{3,4},{4,5},{5,6},{6,7},{7,0},{8,9},{9,10},{10,1... | collective-permute-start | bytes 73736 | tf_op jit(solution)/shard_map/ppermute | solution.py:75
  20.8 15.3 %copy-start.5 = (f32[8,768]{1,0:T(8,128)}, f32[8,768]{1,0:T(8,128)S(1)}, u32[]{:S(2)}) copy-start(f32[8,768]{1,0:T(8,128)S(1)} %collective-permute-done.2) | copy-start | bytes 73732
  20.9 5.0 %collective-permute-start.3 = (f32[8,768]{1,0:T(8,128)S(1)}, f32[8,768]{1,0:T(8,128)S(1)}, u32[]{:S(2)}, u32[]{:S(2)}) collective-permute-start(f32[8,768]{1,0:T(8,128)S(1)} %collective-permute-done.2), channel_id=1, source_target_pairs={{0,1},{1,2},{2,3},{3,4},{4,5},{5,6},{6,7},{7,0},{8,9},{9,10},{10,1... | collective-permute-start | bytes 73736 | tf_op jit(solution)/shard_map/ppermute | solution.py:75
  25.9 10.3 %copy-start.6 = (f32[8,768]{1,0:T(8,128)}, f32[8,768]{1,0:T(8,128)S(1)}, u32[]{:S(2)}) copy-start(f32[8,768]{1,0:T(8,128)S(1)} %collective-permute-done.3) | copy-start | bytes 73732
  25.9 5.0 %collective-permute-start.4 = (f32[8,768]{1,0:T(8,128)S(1)}, f32[8,768]{1,0:T(8,128)S(1)}, u32[]{:S(2)}, u32[]{:S(2)}) collective-permute-start(f32[8,768]{1,0:T(8,128)S(1)} %collective-permute-done.3), channel_id=1, source_target_pairs={{0,1},{1,2},{2,3},{3,4},{4,5},{5,6},{6,7},{7,0},{8,9},{9,10},{10,1... | collective-permute-start | bytes 73736 | tf_op jit(solution)/shard_map/ppermute | solution.py:75
  31.0 5.2 %collective-permute-start.5 = (f32[8,768]{1,0:T(8,128)S(1)}, f32[8,768]{1,0:T(8,128)}, u32[]{:S(2)}, u32[]{:S(2)}) collective-permute-start(f32[8,768]{1,0:T(8,128)S(1)} %collective-permute-done.4), channel_id=1, source_target_pairs={{0,1},{1,2},{2,3},{3,4},{4,5},{5,6},{6,7},{7,0},{8,9},{9,10},{10,1... | collective-permute-start | bytes 73736 | tf_op jit(solution)/shard_map/ppermute | solution.py:75
  36.1 13.8 %collective-permute-start.6 = (f32[8,768]{1,0:T(8,128)}, f32[8,768]{1,0:T(8,128)}, u32[]{:S(2)}, u32[]{:S(2)}) collective-permute-start(f32[8,768]{1,0:T(8,128)} %collective-permute-done.5), channel_id=1, source_target_pairs={{0,1},{1,2},{2,3},{3,4},{4,5},{5,6},{6,7},{7,0},{8,9},{9,10},{10,1... | collective-permute-start | bytes 73736 | tf_op jit(solution)/shard_map/ppermute | solution.py:75
  40.4 32.2 %all-to-all-start.1 = ((f32[32,4,768]{2,1,0:T(4,128)}), f32[32,4,768]{2,1,0:T(4,128)S(1)}, u32[]{:S(2)}, u32[]{:S(2)}) async-start(f32[32,4,768]{2,1,0:T(4,128)} %reshape.135), calls=%async_computation.1 | async-start | bytes 786432 | tf_op jit(solution)/shard_map/all_to_all | solution.py:59
  60.3 21.6 %copy-start.2 = (s32[64,8]{0,1:T(8,128)S(1)}, s32[64,8]{0,1:T(8,128)}, u32[]{:S(2)}) copy-start(s32[64,8]{0,1:T(8,128)} %param.12) | copy-start | bytes 6148
  60.3 21.6 %copy-start.9 = (s32[8]{0:T(128)S(1)}, s32[8]{0:T(128)}, u32[]{:S(2)}) copy-start(s32[8]{0:T(128)} %iota_add_fusion) | copy-start | bytes 100
  75.9 91.5 %all-to-all-start.2 = ((f32[32,1,4]{2,1,0:T(1,128)}), f32[32,1,4]{2,1,0:T(1,128)S(1)}, u32[]{:S(2)}, u32[]{:S(2)}) async-start(f32[32,1,4]{2,1,0:T(1,128)} %copy.33), calls=%async_computation.2 | async-start | bytes 32768 | tf_op jit(solution)/shard_map/all_to_all | solution.py:66
  81.9 6.8 %copy-start.1 = (bf16[64,24576]{1,0:T(8,128)(2,1)S(1)}, bf16[64,24576]{1,0:T(8,128)(2,1)}, u32[]{:S(2)}) copy-start(bf16[64,24576]{1,0:T(8,128)(2,1)} %get-tuple-element.124) | copy-start | bytes 9437188 | tf_op jit(solution)/shard_map/while
  92.6 6.8 %copy-start.1 = (bf16[64,24576]{1,0:T(8,128)(2,1)S(1)}, bf16[64,24576]{1,0:T(8,128)(2,1)}, u32[]{:S(2)}) copy-start(bf16[64,24576]{1,0:T(8,128)(2,1)} %get-tuple-element.124) | copy-start | bytes 9437188 | tf_op jit(solution)/shard_map/while
  103.3 6.8 %copy-start.1 = (bf16[64,24576]{1,0:T(8,128)(2,1)S(1)}, bf16[64,24576]{1,0:T(8,128)(2,1)}, u32[]{:S(2)}) copy-start(bf16[64,24576]{1,0:T(8,128)(2,1)} %get-tuple-element.124) | copy-start | bytes 9437188 | tf_op jit(solution)/shard_map/while
  114.0 6.8 %copy-start.1 = (bf16[64,24576]{1,0:T(8,128)(2,1)S(1)}, bf16[64,24576]{1,0:T(8,128)(2,1)}, u32[]{:S(2)}) copy-start(bf16[64,24576]{1,0:T(8,128)(2,1)} %get-tuple-element.124) | copy-start | bytes 9437188 | tf_op jit(solution)/shard_map/while
  146.0 6.8 %copy-start.1 = (bf16[64,24576]{1,0:T(8,128)(2,1)S(1)}, bf16[64,24576]{1,0:T(8,128)(2,1)}, u32[]{:S(2)}) copy-start(bf16[64,24576]{1,0:T(8,128)(2,1)} %get-tuple-element.124) | copy-start | bytes 9437188 | tf_op jit(solution)/shard_map/while
  156.7 6.8 %copy-start.1 = (bf16[64,24576]{1,0:T(8,128)(2,1)S(1)}, bf16[64,24576]{1,0:T(8,128)(2,1)}, u32[]{:S(2)}) copy-start(bf16[64,24576]{1,0:T(8,128)(2,1)} %get-tuple-element.124) | copy-start | bytes 9437188 | tf_op jit(solution)/shard_map/while
  (3 other events, 18.7 us)
